TPU v7x, 128 devices: a whole 4x4x4 slice. The times are simulated.
128 devices in a mesh: gx: 8 (over y, core), gy: 16 (over z, x).
Axes of the slice: x: 4, y: 4, z: 4, core: 2. Of those that a mesh axis runs over, the one named last changes fastest.
Arguments:
- right_side: float32 [256, 512, 256], P('gx', 'gy'), may hold values from -32 to 32
- phase: int32 [256, 512, 256], P('gx', 'gy'), may hold values from 1 to 3
- table: float32 [4], replicated, may hold values from 0.3 to 3
Outputs:
- solution_field: float32 [256, 512, 256], P('gx', 'gy')
- residual: float32 [256, 512, 256], P('gx', 'gy')
- pre_residual: float32 [256, 512, 256], P('gx', 'gy')
- residual_image: float32 [256, 512, 256], P('gx', 'gy')
Inputs may be any that keep to these rules, and one draw needn't show every extreme that they name: `phase`: labels 1 slag, 2 steel, 3 argon plume; label 0 stands for the lining outside the grid.
All inputs are finite; a program needn't handle non-finite values.
Results may differ from a plain program's by a relative error of at most 0.0003.
Values sent between devices are 32-bit elements; how exact they have to be, the bound alone decides.
No kernel may reach another device: no remote copies, remote signals or barrier semaphores. Data moves between devices by JAX's collectives and lax.ppermute only.
A program may use at most 64 MiB of HBM per device.

v0:
```python
import jax
import jax.numpy as jnp
from jax import lax
from jax.sharding import PartitionSpec as P

ITERS = 2
centre_value = 1.1
half_width = 0.9
ratio_sigma = centre_value / half_width
rho_first = 1.0 / ratio_sigma
rho_second = 1.0 / (2.0 * ratio_sigma - rho_first)
rho_third = 1.0 / (2.0 * ratio_sigma - rho_second)
start_scale = 1.0 / centre_value
keep_first = rho_second * rho_first
push_first = 2.0 * rho_second / half_width
keep_second = rho_third * rho_second
push_second = 2.0 * rho_third / half_width


def extended(block, sides, width):
    for axis, dim in sides:
        count = lax.axis_size(axis)
        forward = [(i, i + 1) for i in range(count - 1)]
        backward = [(target, source) for source, target in forward]
        low = lax.ppermute(
            lax.slice_in_dim(block, block.shape[dim] - width, None, axis=dim), axis, forward
        )
        high = lax.ppermute(lax.slice_in_dim(block, 0, width, axis=dim), axis, backward)
        block = jnp.concatenate([low, block, high], axis=dim)
    return block


def harmonic(left, right):
    return 2.0 * left * right / (left + right)


def coupling_set(sigma_padded):
    centre = sigma_padded[1:-1, 1:-1, 1:-1]
    to_west = harmonic(centre, sigma_padded[:-2, 1:-1, 1:-1])
    to_east = harmonic(centre, sigma_padded[2:, 1:-1, 1:-1])
    to_south = harmonic(centre, sigma_padded[1:-1, :-2, 1:-1])
    to_north = harmonic(centre, sigma_padded[1:-1, 2:, 1:-1])
    to_down = harmonic(centre, sigma_padded[1:-1, 1:-1, :-2])
    to_up = harmonic(centre, sigma_padded[1:-1, 1:-1, 2:])
    diagonal = to_west + to_east + to_south + to_north + to_down + to_up
    return (to_west, to_east, to_south, to_north, to_down, to_up, diagonal)


def lookup(labels, table):
    return jnp.where(
        labels == 1,
        table[1],
        jnp.where(labels == 2, table[2], jnp.where(labels == 3, table[3], table[0])),
    )


def operate_ext(padded_xy, couplings):
    to_west, to_east, to_south, to_north, to_down, to_up, diagonal = couplings
    padded_z = jnp.pad(padded_xy, ((0, 0), (0, 0), (1, 1)))
    centre = padded_xy[1:-1, 1:-1]
    beside = (
        to_west * padded_xy[:-2, 1:-1]
        + to_east * padded_xy[2:, 1:-1]
        + to_south * padded_xy[1:-1, :-2]
        + to_north * padded_xy[1:-1, 2:]
        + to_down * padded_z[1:-1, 1:-1, :-2]
        + to_up * padded_z[1:-1, 1:-1, 2:]
    )
    return diagonal * centre - beside


def local(right_side, phase, table):
    labels_ext = extended(phase, (("gx", 0), ("gy", 1)), 1)
    sigma_ext = lookup(jnp.pad(labels_ext, ((0, 0), (0, 0), (1, 1))), table)
    stored_set = coupling_set(sigma_ext)

    def composite(vector):
        set_zero = tuple((member for member in stored_set))
        diagonal = set_zero[6]

        def image_of(field):
            return operate_ext(extended(field, (("gx", 0), ("gy", 1)), 1), set_zero)

        first = start_scale * (vector / diagonal)
        change = keep_first * first + push_first * ((vector - image_of(first)) / diagonal)
        second = first + change
        change = keep_second * change + push_second * ((vector - image_of(second)) / diagonal)
        third = second + change
        return (third, image_of(third))

    solution_field = jnp.zeros_like(right_side)
    residual = right_side
    pre_residual, residual_image = composite(residual)
    image_dir = jnp.zeros_like(right_side)
    pre_dir = jnp.zeros_like(right_side)
    resid_dir = jnp.zeros_like(right_side)
    direction = jnp.zeros_like(right_side)
    energy_prev = jnp.float32(1.0)
    step_prev = jnp.float32(1.0)
    for iteration in range(ITERS):
        energy_now, curvature = lax.psum(
            (jnp.sum(residual * pre_residual), jnp.sum(residual_image * pre_residual)), ("gx", "gy")
        )
        pre_image, double_image = composite(residual_image)
        if iteration == 0:
            step_size = energy_now / curvature
            image_dir = double_image
            pre_dir = pre_image
            resid_dir = residual_image
            direction = pre_residual
        else:
            momentum = energy_now / energy_prev
            step_size = energy_now / (curvature - momentum * energy_now / step_prev)
            image_dir = double_image + momentum * image_dir
            pre_dir = pre_image + momentum * pre_dir
            resid_dir = residual_image + momentum * resid_dir
            direction = pre_residual + momentum * direction
        solution_field = solution_field + step_size * direction
        residual = residual - step_size * resid_dir
        pre_residual = pre_residual - step_size * pre_dir
        residual_image = residual_image - step_size * image_dir
        energy_prev = energy_now
        step_prev = step_size
    return (solution_field, residual, pre_residual, residual_image)


def solution(mesh):
    placed = (P("gx", "gy", None), P("gx", "gy", None), P())
    return jax.shard_map(
        local,
        mesh=mesh,
        in_specs=placed,
        out_specs=(
            P("gx", "gy", None),
            P("gx", "gy", None),
            P("gx", "gy", None),
            P("gx", "gy", None),
        ),
        check_vma=False,
    )
```

profile of v0, /device:TPU:39, one launch (start us, length us, event | category | flops | bytes accessed | tf_op | source)
XLA Modules:
  0.0 359.8 jit_solution(430377248482108931)
XLA Ops:
  1.4 3.8 %collective-permute-start = (s32[1,32,256]{2,1,0:T(8,128)S(1)}, s32[1,32,256]{2,1,0:T(8,128)S(1)}, u32[]{:S(2)}, u32[]{:S(2)}) collective-permute-start(s32[1,32,256]{2,1,0:T(8,128)S(1)} %get-tuple-element.70), channel_id=1, source_target_pairs={{0,16},{16,32},{32,48},{48,64},{64,80},{80,96},{96,112},{1,17},{17... | collective-permute-start | bytes 98312 | tf_op jit(solution)/shard_map/ppermute | solution.py:25
  10.5 3.5 collective-permute-start.2
  16.5 4.3 %collective-permute-done.3 = s32[34,1,256]{2,1,0:T(1,128)S(1)} collective-permute-done((s32[34,1,256]{2,1,0:T(1,128)S(1)}, s32[34,1,256]{2,1,0:T(1,128)S(1)}, u32[]{:S(2)}, u32[]{:S(2)}) %collective-permute-start.3) | collective-permute-done | bytes 34848 | tf_op jit(solution)/shard_map/ppermute | solution.py:28
  20.9 3.3 select_select_fusion
  26.5 3.3 collective-permute-start.4
  31.8 3.3 collective-permute-done.5
  37.1 3.4 collective-permute-start.7
  40.5 3.4 collective-permute-done.7
  44.8 2.7 fusion.134
  47.6 3.1 collective-permute-start.8
  52.6 3.3 collective-permute-done.9
  57.8 3.4 collective-permute-start.11
  61.2 3.4 collective-permute-done.11
  65.6 2.7 fusion.98
  68.3 3.1 collective-permute-start.12
  73.3 3.3 collective-permute-done.13
  78.6 3.4 collective-permute-start.15
  82.0 3.4 collective-permute-done.15
  86.4 3.3 multiply_reduce_fusion.2
  90.5 3.1 collective-permute-start.16
  95.5 3.3 collective-permute-done.17
  100.8 3.5 collective-permute-start.19
  104.3 3.2 collective-permute-done.19
  111.2 3.1 collective-permute-start.20
  116.2 3.3 collective-permute-done.21
  121.5 3.4 collective-permute-start.23
  124.9 3.4 collective-permute-done.23
  129.3 2.7 fusion.59
  132.0 3.1 collective-permute-start.24
  137.0 3.3 collective-permute-done.25
  142.3 3.4 collective-permute-start.27
  145.7 63.7 %all-reduce.11 = (f32[]{:T(128)}, f32[]{:T(128)}) all-reduce(f32[]{:T(128)} %get-tuple-element.7, f32[]{:T(128)} %get-tuple-element.6), channel_id=1, replica_groups=mesh['gx'=8,'gy'=16] {'gx','gy'}, use_global_device_ids=true, to_apply=%region_1.2 | all-reduce | flops 2 | bytes 16 | tf_op jit(solution)/shard_map/psum | solution.py:101
  213.0 6.4 %fusion.125 = (f32[32,32,256]{2,1,0:T(8,128)S(1)}, f32[32,32,256]{2,1,0:T(8,128)S(1)}, f32[32,32,256]{2,1,0:T(8,128)}) fusion(f32[32,32,256]{2,1,0:T(8,128)S(1)} %copy-done.7, f32[32,32,256]{2,1,0:T(8,128)S(1)} %copy-done.4, f32[32,32,256]{2,1,0:T(8,128)S(1)} %copy-done.1, f32[32,32,256]{2,1,0:T(8,128)S(1)} %get-tuple-element.27, ...), kind=kLoop, calls=%fused_computation.275 | loop fusion | flops 7864320 | bytes 13766660 | tf_op jit(solution)/shard_map/mul | solution.py:84
  219.5 4.5 %collective-permute-start.28 = (f32[1,32,256]{2,1,0:T(8,128)S(1)}, f32[1,32,256]{2,1,0:T(8,128)S(1)}, u32[]{:S(2)}, u32[]{:S(2)}) collective-permute-start(f32[1,32,256]{2,1,0:T(8,128)S(1)} %get-tuple-element.55), channel_id=1, source_target_pairs={{0,16},{16,32},{32,48},{48,64},{64,80},{80,96},{96,112},{1,17},{17... | collective-permute-start | bytes 98312 | tf_op jit(solution)/shard_map/ppermute | solution.py:25
  225.9 3.3 collective-permute-done.29
  229.3 3.3 collective-permute-start.30
  234.6 4.8 %collective-permute-done.31 = f32[34,1,256]{2,1,0:T(1,128)S(1)} collective-permute-done((f32[34,1,256]{2,1,0:T(1,128)S(1)}, f32[34,1,256]{2,1,0:T(1,128)S(1)}, u32[]{:S(2)}, u32[]{:S(2)}) %collective-permute-start.31) | collective-permute-done | bytes 34848 | tf_op jit(solution)/shard_map/ppermute | solution.py:28
  240.4 3.5 fusion.128
  243.9 3.3 collective-permute-start.32
  249.2 3.3 collective-permute-done.33
  254.5 3.6 collective-permute-start.35
  259.3 62.3 %all-reduce.10 = (f32[]{:T(128)}, f32[]{:T(128)}) all-reduce(f32[]{:T(128)} %get-tuple-element.5, f32[]{:T(128)} %get-tuple-element.4), channel_id=1, replica_groups=mesh['gx'=8,'gy'=16] {'gx','gy'}, use_global_device_ids=true, to_apply=%region_5.6 | all-reduce | flops 2 | bytes 16 | tf_op jit(solution)/shard_map/psum | solution.py:101
  328.5 7.3 %multiply_subtract_fusion = (f32[32,32,256]{2,1,0:T(8,128)}, f32[32,32,256]{2,1,0:T(8,128)S(1)}) fusion(f32[32,32,256]{2,1,0:T(8,128)} %copy-done.9, f32[]{:T(128)S(6)} %div.70, f32[]{:T(128)S(6)} %div.72, f32[32,32,256]{2,1,0:T(8,128)} %copy-done.12, f32[]{:T(128)S(6)} %div.66, f32[32,32,256]{2,1,0:T(8,128)} %copy-done.23, f32[32,32,256]{2,1,0:T(8,128)} %copy-done.18, ...), kind=kLoop, calls=%fused_computation.254 | loop fusion | flops 9961472 | bytes 15863820 | tf_op jit(solution)/shard_map/sub | solution.py:120
  335.7 4.2 %collective-permute-start.36 = (f32[1,32,256]{2,1,0:T(8,128)S(1)}, f32[1,32,256]{2,1,0:T(8,128)S(1)}, u32[]{:S(2)}, u32[]{:S(2)}) collective-permute-start(f32[1,32,256]{2,1,0:T(8,128)S(1)} %get-tuple-element.51), channel_id=1, source_target_pairs={{0,16},{16,32},{32,48},{48,64},{64,80},{80,96},{96,112},{1,17},{17... | collective-permute-start | bytes 98312 | tf_op jit(solution)/shard_map/ppermute | solution.py:25
  341.8 3.3 collective-permute-done.37
  345.2 3.3 collective-permute-start.38
  352.5 2.8 collective-permute-done.39
  356.3 3.5 fusion.5
  (134 shorter events, 64.1 us)
Async XLA Ops:
  1.4 5.7 %collective-permute-start = (s32[1,32,256]{2,1,0:T(8,128)S(1)}, s32[1,32,256]{2,1,0:T(8,128)S(1)}, u32[]{:S(2)}, u32[]{:S(2)}) collective-permute-start(s32[1,32,256]{2,1,0:T(8,128)S(1)} %get-tuple-element.70), channel_id=1, source_target_pairs={{0,16},{16,32},{32,48},{48,64},{64,80},{80,96},{96,112},{1,17},{17... | collective-permute-start | bytes 98312 | tf_op jit(solution)/shard_map/ppermute | solution.py:25
  5.2 5.2 %collective-permute-start.1 = (s32[1,32,256]{2,1,0:T(8,128)S(1)}, s32[1,32,256]{2,1,0:T(8,128)S(1)}, u32[]{:S(2)}, u32[]{:S(2)}) collective-permute-start(s32[1,32,256]{2,1,0:T(8,128)S(1)} %get-tuple-element.69), channel_id=1, source_target_pairs={{16,0},{32,16},{48,32},{64,48},{80,64},{96,80},{112,96},{17,1},{33... | collective-permute-start | bytes 98312 | tf_op jit(solution)/shard_map/ppermute | solution.py:28
  10.5 6.0 %collective-permute-start.2 = (s32[34,1,256]{2,1,0:T(1,128)S(1)}, s32[34,1,256]{2,1,0:T(1,128)S(1)}, u32[]{:S(2)}, u32[]{:S(2)}) collective-permute-start(s32[34,1,256]{2,1,0:T(1,128)S(1)} %get-tuple-element.49), channel_id=1, source_target_pairs={{0,1},{1,2},{2,3},{3,4},{4,5},{5,6},{6,7},{7,8},{8,9},{9,10},{10,1... | collective-permute-start | bytes 104456 | tf_op jit(solution)/shard_map/ppermute | solution.py:25
  13.9 6.8 %collective-permute-start.3 = (s32[34,1,256]{2,1,0:T(1,128)S(1)}, s32[34,1,256]{2,1,0:T(1,128)S(1)}, u32[]{:S(2)}, u32[]{:S(2)}) collective-permute-start(s32[34,1,256]{2,1,0:T(1,128)S(1)} %get-tuple-element.50), channel_id=1, source_target_pairs={{1,0},{2,1},{3,2},{4,3},{5,4},{6,5},{7,6},{8,7},{9,8},{10,9},{11,1... | collective-permute-start | bytes 104456 | tf_op jit(solution)/shard_map/ppermute | solution.py:28
  26.5 102.7 %copy-start = (f32[32,32,256]{2,1,0:T(8,128)}, f32[32,32,256]{2,1,0:T(8,128)S(1)}, u32[]{:S(2)}) copy-start(f32[32,32,256]{2,1,0:T(8,128)S(1)} %get-tuple-element.28) | copy-start | bytes 3145732
  26.5 102.7 %copy-start.3 = (f32[32,32,256]{2,1,0:T(8,128)}, f32[32,32,256]{2,1,0:T(8,128)S(1)}, u32[]{:S(2)}) copy-start(f32[32,32,256]{2,1,0:T(8,128)S(1)} %get-tuple-element.29) | copy-start | bytes 3145732
  26.5 102.7 %copy-start.6 = (f32[32,32,256]{2,1,0:T(8,128)}, f32[32,32,256]{2,1,0:T(8,128)S(1)}, u32[]{:S(2)}) copy-start(f32[32,32,256]{2,1,0:T(8,128)S(1)} %get-tuple-element.30) | copy-start | bytes 3145732
  26.5 5.3 %collective-permute-start.4 = (f32[1,32,256]{2,1,0:T(8,128)S(1)}, f32[1,32,256]{2,1,0:T(8,128)S(1)}, u32[]{:S(2)}, u32[]{:S(2)}) collective-permute-start(f32[1,32,256]{2,1,0:T(8,128)S(1)} %get-tuple-element.67), channel_id=1, source_target_pairs={{0,16},{16,32},{32,48},{48,64},{64,80},{80,96},{96,112},{1,17},{17... | collective-permute-start | bytes 98312 | tf_op jit(solution)/shard_map/ppermute | solution.py:25
  29.9 5.2 %collective-permute-start.5 = (f32[1,32,256]{2,1,0:T(8,128)S(1)}, f32[1,32,256]{2,1,0:T(8,128)S(1)}, u32[]{:S(2)}, u32[]{:S(2)}) collective-permute-start(f32[1,32,256]{2,1,0:T(8,128)S(1)} %get-tuple-element.68), channel_id=1, source_target_pairs={{16,0},{32,16},{48,32},{64,48},{80,64},{96,80},{112,96},{17,1},{33... | collective-permute-start | bytes 98312 | tf_op jit(solution)/shard_map/ppermute | solution.py:28
  35.2 5.3 %collective-permute-start.6 = (f32[34,1,256]{2,1,0:T(1,128)S(1)}, f32[34,1,256]{2,1,0:T(1,128)S(1)}, u32[]{:S(2)}, u32[]{:S(2)}) collective-permute-start(f32[34,1,256]{2,1,0:T(1,128)S(1)} %get-tuple-element.47), channel_id=1, source_target_pairs={{0,1},{1,2},{2,3},{3,4},{4,5},{5,6},{6,7},{7,8},{8,9},{9,10},{10,1... | collective-permute-start | bytes 104456 | tf_op jit(solution)/shard_map/ppermute | solution.py:25
  37.1 6.8 %collective-permute-start.7 = (f32[34,1,256]{2,1,0:T(1,128)S(1)}, f32[34,1,256]{2,1,0:T(1,128)S(1)}, u32[]{:S(2)}, u32[]{:S(2)}) collective-permute-start(f32[34,1,256]{2,1,0:T(1,128)S(1)} %get-tuple-element.48), channel_id=1, source_target_pairs={{1,0},{2,1},{3,2},{4,3},{5,4},{6,5},{7,6},{8,7},{9,8},{10,9},{11,1... | collective-permute-start | bytes 104456 | tf_op jit(solution)/shard_map/ppermute | solution.py:28
  47.6 5.0 %collective-permute-start.8 = (f32[1,32,256]{2,1,0:T(8,128)S(1)}, f32[1,32,256]{2,1,0:T(8,128)S(1)}, u32[]{:S(2)}, u32[]{:S(2)}) collective-permute-start(f32[1,32,256]{2,1,0:T(8,128)S(1)} %get-tuple-element.65), channel_id=1, source_target_pairs={{0,16},{16,32},{32,48},{48,64},{64,80},{80,96},{96,112},{1,17},{17... | collective-permute-start | bytes 98312 | tf_op jit(solution)/shard_map/ppermute | solution.py:25
  50.6 5.2 %collective-permute-start.9 = (f32[1,32,256]{2,1,0:T(8,128)S(1)}, f32[1,32,256]{2,1,0:T(8,128)S(1)}, u32[]{:S(2)}, u32[]{:S(2)}) collective-permute-start(f32[1,32,256]{2,1,0:T(8,128)S(1)} %get-tuple-element.66), channel_id=1, source_target_pairs={{16,0},{32,16},{48,32},{64,48},{80,64},{96,80},{112,96},{17,1},{33... | collective-permute-start | bytes 98312 | tf_op jit(solution)/shard_map/ppermute | solution.py:28
  55.9 5.3 %collective-permute-start.10 = (f32[34,1,256]{2,1,0:T(1,128)S(1)}, f32[34,1,256]{2,1,0:T(1,128)S(1)}, u32[]{:S(2)}, u32[]{:S(2)}) collective-permute-start(f32[34,1,256]{2,1,0:T(1,128)S(1)} %get-tuple-element.45), channel_id=1, source_target_pairs={{0,1},{1,2},{2,3},{3,4},{4,5},{5,6},{6,7},{7,8},{8,9},{9,10},{10,1... | collective-permute-start | bytes 104456 | tf_op jit(solution)/shard_map/ppermute | solution.py:25
  57.8 6.8 %collective-permute-start.11 = (f32[34,1,256]{2,1,0:T(1,128)S(1)}, f32[34,1,256]{2,1,0:T(1,128)S(1)}, u32[]{:S(2)}, u32[]{:S(2)}) collective-permute-start(f32[34,1,256]{2,1,0:T(1,128)S(1)} %get-tuple-element.46), channel_id=1, source_target_pairs={{1,0},{2,1},{3,2},{4,3},{5,4},{6,5},{7,6},{8,7},{9,8},{10,9},{11,1... | collective-permute-start | bytes 104456 | tf_op jit(solution)/shard_map/ppermute | solution.py:28
  68.3 5.0 %collective-permute-start.12 = (f32[1,32,256]{2,1,0:T(8,128)S(1)}, f32[1,32,256]{2,1,0:T(8,128)S(1)}, u32[]{:S(2)}, u32[]{:S(2)}) collective-permute-start(f32[1,32,256]{2,1,0:T(8,128)S(1)} %get-tuple-element.63), channel_id=1, source_target_pairs={{0,16},{16,32},{32,48},{48,64},{64,80},{80,96},{96,112},{1,17},{17... | collective-permute-start | bytes 98312 | tf_op jit(solution)/shard_map/ppermute | solution.py:25
  71.4 5.2 %collective-permute-start.13 = (f32[1,32,256]{2,1,0:T(8,128)S(1)}, f32[1,32,256]{2,1,0:T(8,128)S(1)}, u32[]{:S(2)}, u32[]{:S(2)}) collective-permute-start(f32[1,32,256]{2,1,0:T(8,128)S(1)} %get-tuple-element.64), channel_id=1, source_target_pairs={{16,0},{32,16},{48,32},{64,48},{80,64},{96,80},{112,96},{17,1},{33... | collective-permute-start | bytes 98312 | tf_op jit(solution)/shard_map/ppermute | solution.py:28
  76.7 5.3 %collective-permute-start.14 = (f32[34,1,256]{2,1,0:T(1,128)S(1)}, f32[34,1,256]{2,1,0:T(1,128)S(1)}, u32[]{:S(2)}, u32[]{:S(2)}) collective-permute-start(f32[34,1,256]{2,1,0:T(1,128)S(1)} %get-tuple-element.43), channel_id=1, source_target_pairs={{0,1},{1,2},{2,3},{3,4},{4,5},{5,6},{6,7},{7,8},{8,9},{9,10},{10,1... | collective-permute-start | bytes 104456 | tf_op jit(solution)/shard_map/ppermute | solution.py:25
  78.6 6.8 %collective-permute-start.15 = (f32[34,1,256]{2,1,0:T(1,128)S(1)}, f32[34,1,256]{2,1,0:T(1,128)S(1)}, u32[]{:S(2)}, u32[]{:S(2)}) collective-permute-start(f32[34,1,256]{2,1,0:T(1,128)S(1)} %get-tuple-element.44), channel_id=1, source_target_pairs={{1,0},{2,1},{3,2},{4,3},{5,4},{6,5},{7,6},{8,7},{9,8},{10,9},{11,1... | collective-permute-start | bytes 104456 | tf_op jit(solution)/shard_map/ppermute | solution.py:28
  89.6 39.6 %copy-start.15 = (f32[32,32,256]{2,1,0:T(8,128)}, f32[32,32,256]{2,1,0:T(8,128)S(1)}, u32[]{:S(2)}) copy-start(f32[32,32,256]{2,1,0:T(8,128)S(1)} %get-tuple-element.19) | copy-start | bytes 3145732
  90.5 5.0 %collective-permute-start.16 = (f32[1,32,256]{2,1,0:T(8,128)S(1)}, f32[1,32,256]{2,1,0:T(8,128)S(1)}, u32[]{:S(2)}, u32[]{:S(2)}) collective-permute-start(f32[1,32,256]{2,1,0:T(8,128)S(1)} %get-tuple-element.61), channel_id=1, source_target_pairs={{0,16},{16,32},{32,48},{48,64},{64,80},{80,96},{96,112},{1,17},{17... | collective-permute-start | bytes 98312 | tf_op jit(solution)/shard_map/ppermute | solution.py:25
  93.6 5.2 %collective-permute-start.17 = (f32[1,32,256]{2,1,0:T(8,128)S(1)}, f32[1,32,256]{2,1,0:T(8,128)S(1)}, u32[]{:S(2)}, u32[]{:S(2)}) collective-permute-start(f32[1,32,256]{2,1,0:T(8,128)S(1)} %get-tuple-element.62), channel_id=1, source_target_pairs={{16,0},{32,16},{48,32},{64,48},{80,64},{96,80},{112,96},{17,1},{33... | collective-permute-start | bytes 98312 | tf_op jit(solution)/shard_map/ppermute | solution.py:28
  98.8 5.5 %collective-permute-start.18 = (f32[34,1,256]{2,1,0:T(1,128)S(1)}, f32[34,1,256]{2,1,0:T(1,128)S(1)}, u32[]{:S(2)}, u32[]{:S(2)}) collective-permute-start(f32[34,1,256]{2,1,0:T(1,128)S(1)} %get-tuple-element.41), channel_id=1, source_target_pairs={{0,1},{1,2},{2,3},{3,4},{4,5},{5,6},{6,7},{7,8},{8,9},{9,10},{10,1... | collective-permute-start | bytes 104456 | tf_op jit(solution)/shard_map/ppermute | solution.py:25
  100.8 6.8 %collective-permute-start.19 = (f32[34,1,256]{2,1,0:T(1,128)S(1)}, f32[34,1,256]{2,1,0:T(1,128)S(1)}, u32[]{:S(2)}, u32[]{:S(2)}) collective-permute-start(f32[34,1,256]{2,1,0:T(1,128)S(1)} %get-tuple-element.42), channel_id=1, source_target_pairs={{1,0},{2,1},{3,2},{4,3},{5,4},{6,5},{7,6},{8,7},{9,8},{10,9},{11,1... | collective-permute-start | bytes 104456 | tf_op jit(solution)/shard_map/ppermute | solution.py:28
  111.2 5.0 %collective-permute-start.20 = (f32[1,32,256]{2,1,0:T(8,128)S(1)}, f32[1,32,256]{2,1,0:T(8,128)S(1)}, u32[]{:S(2)}, u32[]{:S(2)}) collective-permute-start(f32[1,32,256]{2,1,0:T(8,128)S(1)} %get-tuple-element.59), channel_id=1, source_target_pairs={{0,16},{16,32},{32,48},{48,64},{64,80},{80,96},{96,112},{1,17},{17... | collective-permute-start | bytes 98312 | tf_op jit(solution)/shard_map/ppermute | solution.py:25
  114.3 5.2 %collective-permute-start.21 = (f32[1,32,256]{2,1,0:T(8,128)S(1)}, f32[1,32,256]{2,1,0:T(8,128)S(1)}, u32[]{:S(2)}, u32[]{:S(2)}) collective-permute-start(f32[1,32,256]{2,1,0:T(8,128)S(1)} %get-tuple-element.60), channel_id=1, source_target_pairs={{16,0},{32,16},{48,32},{64,48},{80,64},{96,80},{112,96},{17,1},{33... | collective-permute-start | bytes 98312 | tf_op jit(solution)/shard_map/ppermute | solution.py:28
  119.6 5.3 %collective-permute-start.22 = (f32[34,1,256]{2,1,0:T(1,128)S(1)}, f32[34,1,256]{2,1,0:T(1,128)S(1)}, u32[]{:S(2)}, u32[]{:S(2)}) collective-permute-start(f32[34,1,256]{2,1,0:T(1,128)S(1)} %get-tuple-element.39), channel_id=1, source_target_pairs={{0,1},{1,2},{2,3},{3,4},{4,5},{5,6},{6,7},{7,8},{8,9},{9,10},{10,1... | collective-permute-start | bytes 104456 | tf_op jit(solution)/shard_map/ppermute | solution.py:25
  121.5 6.8 %collective-permute-start.23 = (f32[34,1,256]{2,1,0:T(1,128)S(1)}, f32[34,1,256]{2,1,0:T(1,128)S(1)}, u32[]{:S(2)}, u32[]{:S(2)}) collective-permute-start(f32[34,1,256]{2,1,0:T(1,128)S(1)} %get-tuple-element.40), channel_id=1, source_target_pairs={{1,0},{2,1},{3,2},{4,3},{5,4},{6,5},{7,6},{8,7},{9,8},{10,9},{11,1... | collective-permute-start | bytes 104456 | tf_op jit(solution)/shard_map/ppermute | solution.py:28
  132.0 5.0 %collective-permute-start.24 = (f32[1,32,256]{2,1,0:T(8,128)S(1)}, f32[1,32,256]{2,1,0:T(8,128)S(1)}, u32[]{:S(2)}, u32[]{:S(2)}) collective-permute-start(f32[1,32,256]{2,1,0:T(8,128)S(1)} %get-tuple-element.57), channel_id=1, source_target_pairs={{0,16},{16,32},{32,48},{48,64},{64,80},{80,96},{96,112},{1,17},{17... | collective-permute-start | bytes 98312 | tf_op jit(solution)/shard_map/ppermute | solution.py:25
  135.1 5.2 %collective-permute-start.25 = (f32[1,32,256]{2,1,0:T(8,128)S(1)}, f32[1,32,256]{2,1,0:T(8,128)S(1)}, u32[]{:S(2)}, u32[]{:S(2)}) collective-permute-start(f32[1,32,256]{2,1,0:T(8,128)S(1)} %get-tuple-element.58), channel_id=1, source_target_pairs={{16,0},{32,16},{48,32},{64,48},{80,64},{96,80},{112,96},{17,1},{33... | collective-permute-start | bytes 98312 | tf_op jit(solution)/shard_map/ppermute | solution.py:28
  140.4 70.3 %collective-permute-start.26 = (f32[34,1,256]{2,1,0:T(1,128)S(1)}, f32[34,1,256]{2,1,0:T(1,128)S(1)}, u32[]{:S(2)}, u32[]{:S(2)}) collective-permute-start(f32[34,1,256]{2,1,0:T(1,128)S(1)} %get-tuple-element.37), channel_id=1, source_target_pairs={{0,1},{1,2},{2,3},{3,4},{4,5},{5,6},{6,7},{7,8},{8,9},{9,10},{10,1... | collective-permute-start | bytes 104456 | tf_op jit(solution)/shard_map/ppermute | solution.py:25
  142.3 68.4 %collective-permute-start.27 = (f32[34,1,256]{2,1,0:T(1,128)S(1)}, f32[34,1,256]{2,1,0:T(1,128)S(1)}, u32[]{:S(2)}, u32[]{:S(2)}) collective-permute-start(f32[34,1,256]{2,1,0:T(1,128)S(1)} %get-tuple-element.38), channel_id=1, source_target_pairs={{1,0},{2,1},{3,2},{4,3},{5,4},{6,5},{7,6},{8,7},{9,8},{10,9},{11,1... | collective-permute-start | bytes 104456 | tf_op jit(solution)/shard_map/ppermute | solution.py:28
  219.5 38.6 %copy-start.18 = (f32[32,32,256]{2,1,0:T(8,128)}, f32[32,32,256]{2,1,0:T(8,128)S(1)}, u32[]{:S(2)}) copy-start(f32[32,32,256]{2,1,0:T(8,128)S(1)} %get-tuple-element.17) | copy-start | bytes 3145732
  219.5 6.4 %collective-permute-start.28 = (f32[1,32,256]{2,1,0:T(8,128)S(1)}, f32[1,32,256]{2,1,0:T(8,128)S(1)}, u32[]{:S(2)}, u32[]{:S(2)}) collective-permute-start(f32[1,32,256]{2,1,0:T(8,128)S(1)} %get-tuple-element.55), channel_id=1, source_target_pairs={{0,16},{16,32},{32,48},{48,64},{64,80},{80,96},{96,112},{1,17},{17... | collective-permute-start | bytes 98312 | tf_op jit(solution)/shard_map/ppermute | solution.py:25
  224.0 5.2 %collective-permute-start.29 = (f32[1,32,256]{2,1,0:T(8,128)S(1)}, f32[1,32,256]{2,1,0:T(8,128)S(1)}, u32[]{:S(2)}, u32[]{:S(2)}) collective-permute-start(f32[1,32,256]{2,1,0:T(8,128)S(1)} %get-tuple-element.56), channel_id=1, source_target_pairs={{16,0},{32,16},{48,32},{64,48},{80,64},{96,80},{112,96},{17,1},{33... | collective-permute-start | bytes 98312 | tf_op jit(solution)/shard_map/ppermute | solution.py:28
  229.3 5.3 %collective-permute-start.30 = (f32[34,1,256]{2,1,0:T(1,128)S(1)}, f32[34,1,256]{2,1,0:T(1,128)S(1)}, u32[]{:S(2)}, u32[]{:S(2)}) collective-permute-start(f32[34,1,256]{2,1,0:T(1,128)S(1)} %get-tuple-element.35), channel_id=1, source_target_pairs={{0,1},{1,2},{2,3},{3,4},{4,5},{5,6},{6,7},{7,8},{8,9},{9,10},{10,1... | collective-permute-start | bytes 104456 | tf_op jit(solution)/shard_map/ppermute | solution.py:25
  232.6 6.8 %collective-permute-start.31 = (f32[34,1,256]{2,1,0:T(1,128)S(1)}, f32[34,1,256]{2,1,0:T(1,128)S(1)}, u32[]{:S(2)}, u32[]{:S(2)}) collective-permute-start(f32[34,1,256]{2,1,0:T(1,128)S(1)} %get-tuple-element.36), channel_id=1, source_target_pairs={{1,0},{2,1},{3,2},{4,3},{5,4},{6,5},{7,6},{8,7},{9,8},{10,9},{11,1... | collective-permute-start | bytes 104456 | tf_op jit(solution)/shard_map/ppermute | solution.py:28
  243.9 5.3 %collective-permute-start.32 = (f32[1,32,256]{2,1,0:T(8,128)S(1)}, f32[1,32,256]{2,1,0:T(8,128)S(1)}, u32[]{:S(2)}, u32[]{:S(2)}) collective-permute-start(f32[1,32,256]{2,1,0:T(8,128)S(1)} %get-tuple-element.53), channel_id=1, source_target_pairs={{0,16},{16,32},{32,48},{48,64},{64,80},{80,96},{96,112},{1,17},{17... | collective-permute-start | bytes 98312 | tf_op jit(solution)/shard_map/ppermute | solution.py:25
  247.3 5.2 %collective-permute-start.33 = (f32[1,32,256]{2,1,0:T(8,128)S(1)}, f32[1,32,256]{2,1,0:T(8,128)S(1)}, u32[]{:S(2)}, u32[]{:S(2)}) collective-permute-start(f32[1,32,256]{2,1,0:T(8,128)S(1)} %get-tuple-element.54), channel_id=1, source_target_pairs={{16,0},{32,16},{48,32},{64,48},{80,64},{96,80},{112,96},{17,1},{33... | collective-permute-start | bytes 98312 | tf_op jit(solution)/shard_map/ppermute | solution.py:28
  252.6 73.5 %collective-permute-start.34 = (f32[34,1,256]{2,1,0:T(1,128)S(1)}, f32[34,1,256]{2,1,0:T(1,128)S(1)}, u32[]{:S(2)}, u32[]{:S(2)}) collective-permute-start(f32[34,1,256]{2,1,0:T(1,128)S(1)} %get-tuple-element.33), channel_id=1, source_target_pairs={{0,1},{1,2},{2,3},{3,4},{4,5},{5,6},{6,7},{7,8},{8,9},{9,10},{10,1... | collective-permute-start | bytes 104456 | tf_op jit(solution)/shard_map/ppermute | solution.py:25
  254.5 71.6 %collective-permute-start.35 = (f32[34,1,256]{2,1,0:T(1,128)S(1)}, f32[34,1,256]{2,1,0:T(1,128)S(1)}, u32[]{:S(2)}, u32[]{:S(2)}) collective-permute-start(f32[34,1,256]{2,1,0:T(1,128)S(1)} %get-tuple-element.34), channel_id=1, source_target_pairs={{1,0},{2,1},{3,2},{4,3},{5,4},{6,5},{7,6},{8,7},{9,8},{10,9},{11,1... | collective-permute-start | bytes 104456 | tf_op jit(solution)/shard_map/ppermute | solution.py:28
  328.4 22.1 %copy-start.11 = (f32[32,32,256]{2,1,0:T(8,128)S(1)}, f32[32,32,256]{2,1,0:T(8,128)}, u32[]{:S(2)}) copy-start(f32[32,32,256]{2,1,0:T(8,128)} %copy-done.9) | copy-start | bytes 3145732
  328.4 22.1 %copy-start.14 = (f32[32,32,256]{2,1,0:T(8,128)S(1)}, f32[32,32,256]{2,1,0:T(8,128)}, u32[]{:S(2)}) copy-start(f32[32,32,256]{2,1,0:T(8,128)} %copy-done.12) | copy-start | bytes 3145732
  328.4 22.1 %copy-start.17 = (f32[32,32,256]{2,1,0:T(8,128)S(1)}, f32[32,32,256]{2,1,0:T(8,128)}, u32[]{:S(2)}) copy-start(f32[32,32,256]{2,1,0:T(8,128)} %copy-done.15) | copy-start | bytes 3145732
  335.7 6.1 %collective-permute-start.36 = (f32[1,32,256]{2,1,0:T(8,128)S(1)}, f32[1,32,256]{2,1,0:T(8,128)S(1)}, u32[]{:S(2)}, u32[]{:S(2)}) collective-permute-start(f32[1,32,256]{2,1,0:T(8,128)S(1)} %get-tuple-element.51), channel_id=1, source_target_pairs={{0,16},{16,32},{32,48},{48,64},{64,80},{80,96},{96,112},{1,17},{17... | collective-permute-start | bytes 98312 | tf_op jit(solution)/shard_map/ppermute | solution.py:25
  339.9 5.2 %collective-permute-start.37 = (f32[1,32,256]{2,1,0:T(8,128)S(1)}, f32[1,32,256]{2,1,0:T(8,128)S(1)}, u32[]{:S(2)}, u32[]{:S(2)}) collective-permute-start(f32[1,32,256]{2,1,0:T(8,128)S(1)} %get-tuple-element.52), channel_id=1, source_target_pairs={{16,0},{32,16},{48,32},{64,48},{80,64},{96,80},{112,96},{17,1},{33... | collective-permute-start | bytes 98312 | tf_op jit(solution)/shard_map/ppermute | solution.py:28
  345.2 7.3 %collective-permute-start.38 = (f32[34,1,256]{2,1,0:T(1,128)S(1)}, f32[34,1,256]{2,1,0:T(1,128)S(1)}, u32[]{:S(2)}, u32[]{:S(2)}) collective-permute-start(f32[34,1,256]{2,1,0:T(1,128)S(1)} %get-tuple-element.31), channel_id=1, source_target_pairs={{0,1},{1,2},{2,3},{3,4},{4,5},{5,6},{6,7},{7,8},{8,9},{9,10},{10,1... | collective-permute-start | bytes 104456 | tf_op jit(solution)/shard_map/ppermute | solution.py:25
  348.5 6.8 %collective-permute-start.39 = (f32[34,1,256]{2,1,0:T(1,128)S(1)}, f32[34,1,256]{2,1,0:T(1,128)S(1)}, u32[]{:S(2)}, u32[]{:S(2)}) collective-permute-start(f32[34,1,256]{2,1,0:T(1,128)S(1)} %get-tuple-element.32), channel_id=1, source_target_pairs={{1,0},{2,1},{3,2},{4,3},{5,4},{6,5},{7,6},{8,7},{9,8},{10,9},{11,1... | collective-permute-start | bytes 104456 | tf_op jit(solution)/shard_map/ppermute | solution.py:28
  (18 other events, 193.4 us)
where the time goes:
time: 361 us; the launch traced here: 360 us
  blocking collectives  126 us (35%)
  starting transfers between devices  107 us (30%)
  waiting for transfers between devices  60.4 us (17%)
  other arithmetic  56.1 us (16%)
  between operations  7.42 us (2%)
    psum x2, blocking collectives, local(): lax.psum((jnp.sum(residual * pre_residual), jnp.sum(residual_image * pre_...  126 us
    ppermute x20, waiting for transfers between devices, extended(): lax.ppermute(lax.slice_in_dim(block, 0, width, axis=dim), axis, backward)  60.4 us
    ppermute x20, starting transfers between devices, extended(): lax.ppermute(lax.slice_in_dim(block, block.shape[dim] - width, None, axis...  57.9 us
    ppermute x20, starting transfers between devices, extended(): lax.ppermute(lax.slice_in_dim(block, 0, width, axis=dim), axis, backward)  49 us
    concatenate x10, other arithmetic, extended(): block = jnp.concatenate([low, block, high], axis=dim)  11.3 us
    mul x3, other arithmetic, composite(): first = start_scale * (vector / diagonal)  9.5 us
    add x3, other arithmetic, composite(): second = first + change  8.92 us
    sub x1, other arithmetic, local(): pre_residual = pre_residual - step_size * pre_dir  7.26 us
  transfers between devices with their start and end apart: 40, of which 18 were waited for; matrix products, arithmetic and copies ran while one was open for 1% of the time, Pallas kernels for 0%

commit v1 on v0

--- a/solution.py
+++ b/solution.py
@@ -98,8 +98,9 @@
     energy_prev = jnp.float32(1.0)
     step_prev = jnp.float32(1.0)
     for iteration in range(ITERS):
-        energy_now, curvature = lax.psum(
-            (jnp.sum(residual * pre_residual), jnp.sum(residual_image * pre_residual)), ("gx", "gy")
+        racks_write = lambda piece_in: lax.psum(lax.psum(piece_in, "gx"), "gy")
+        energy_now, curvature = racks_write(
+            (jnp.sum(residual * pre_residual), jnp.sum(residual_image * pre_residual))
         )
         pre_image, double_image = composite(residual_image)
         if iteration == 0:

time: 361 us -> 325 us (0.900)
  blocking collectives: 126 us -> 71.7 us
  starting transfers between devices: 107 us -> 124 us
    psum x2 -> x4, blocking collectives: 126 us -> 71.7 us  [local(): racks_write = lambda piece_in: lax.psum(lax.psum(piece_in, 'gx'), 'gy')]
    ppermute x20, starting transfers between devices: 57.9 us -> 75.3 us  [extended(): lax.ppermute(lax.slice_in_dim(block, block.shape[dim] - width, None, axis...]
  transfers between devices with their start and end apart: 40 -> 40, of which waited for: 18 -> 18; matrix products, arithmetic and copies ran while one was open for 1% -> 2% of each run, Pallas kernels for 0% -> 0%
where the time goes in v1:
time: 325 us; the launch traced here: 323 us
  starting transfers between devices  124 us (38%)
  blocking collectives  71.7 us (22%)
  waiting for transfers between devices  60.1 us (18%)
  other arithmetic  56.4 us (17%)
  between operations  7.72 us (2%)
    ppermute x20, starting transfers between devices, extended(): lax.ppermute(lax.slice_in_dim(block, block.shape[dim] - width, None, axis...  75.3 us
    psum x4, blocking collectives, local(): racks_write = lambda piece_in: lax.psum(lax.psum(piece_in, 'gx'), 'gy')  71.7 us
    ppermute x20, waiting for transfers between devices, extended(): lax.ppermute(lax.slice_in_dim(block, 0, width, axis=dim), axis, backward)  60.1 us
    ppermute x20, starting transfers between devices, extended(): lax.ppermute(lax.slice_in_dim(block, 0, width, axis=dim), axis, backward)  49.1 us
    concatenate x10, other arithmetic, extended(): block = jnp.concatenate([low, block, high], axis=dim)  11.3 us
    mul x3, other arithmetic, composite(): first = start_scale * (vector / diagonal)  9.67 us
    add x3, other arithmetic, composite(): second = first + change  8.9 us
    sub x1, other arithmetic, local(): pre_residual = pre_residual - step_size * pre_dir  7.45 us
  transfers between devices with their start and end apart: 40, of which 18 were waited for; matrix products, arithmetic and copies ran while one was open for 2% of the time, Pallas kernels for 0%

profile of v1, /device:TPU:39, one launch (start us, length us, event | category | flops | bytes accessed | tf_op | source)
XLA Modules:
  0.0 323.3 jit_solution(4925745602213888747)
XLA Ops:
  1.4 3.8 %collective-permute-start = (s32[1,32,256]{2,1,0:T(8,128)S(1)}, s32[1,32,256]{2,1,0:T(8,128)S(1)}, u32[]{:S(2)}, u32[]{:S(2)}) collective-permute-start(s32[1,32,256]{2,1,0:T(8,128)S(1)} %get-tuple-element.74), channel_id=1, source_target_pairs={{0,16},{16,32},{32,48},{48,64},{64,80},{80,96},{96,112},{1,17},{17... | collective-permute-start | bytes 98312 | tf_op jit(solution)/shard_map/ppermute | solution.py:25
  10.5 3.5 %collective-permute-start.2 = (s32[34,1,256]{2,1,0:T(1,128)S(1)}, s32[34,1,256]{2,1,0:T(1,128)S(1)}, u32[]{:S(2)}, u32[]{:S(2)}) collective-permute-start(s32[34,1,256]{2,1,0:T(1,128)S(1)} %get-tuple-element.53), channel_id=1, source_target_pairs={{0,1},{1,2},{2,3},{3,4},{4,5},{5,6},{6,7},{7,8},{8,9},{9,10},{10,1... | collective-permute-start | bytes 104456 | tf_op jit(solution)/shard_map/ppermute | solution.py:25
  16.5 4.3 %collective-permute-done.3 = s32[34,1,256]{2,1,0:T(1,128)S(1)} collective-permute-done((s32[34,1,256]{2,1,0:T(1,128)S(1)}, s32[34,1,256]{2,1,0:T(1,128)S(1)}, u32[]{:S(2)}, u32[]{:S(2)}) %collective-permute-start.3) | collective-permute-done | bytes 34848 | tf_op jit(solution)/shard_map/ppermute | solution.py:28
  20.9 3.3 %select_select_fusion = f32[34,34,258]{2,1,0:T(8,128)S(1)} fusion(s32[34,34,256]{2,1,0:T(8,128)S(1)} %pad_add_fusion, f32[]{:T(128)} %bitcast.3, f32[]{:T(128)} %bitcast.2, f32[]{:T(128)} %bitcast.1, f32[]{:T(128)} %bitcast), kind=kLoop, calls=%fused_computation.41 | loop fusion | flops 1789488 | bytes 2376752 | tf_op jit(solution)/shard_map/jit(_where)/select_n | solution.py:50
  26.5 3.3 %collective-permute-start.4 = (f32[1,32,256]{2,1,0:T(8,128)S(1)}, f32[1,32,256]{2,1,0:T(8,128)S(1)}, u32[]{:S(2)}, u32[]{:S(2)}) collective-permute-start(f32[1,32,256]{2,1,0:T(8,128)S(1)} %get-tuple-element.71), channel_id=1, source_target_pairs={{0,16},{16,32},{32,48},{48,64},{64,80},{80,96},{96,112},{1,17},{17... | collective-permute-start | bytes 98312 | tf_op jit(solution)/shard_map/ppermute | solution.py:25
  31.8 3.3 %collective-permute-done.5 = f32[1,32,256]{2,1,0:T(8,128)S(1)} collective-permute-done((f32[1,32,256]{2,1,0:T(8,128)S(1)}, f32[1,32,256]{2,1,0:T(8,128)S(1)}, u32[]{:S(2)}, u32[]{:S(2)}) %collective-permute-start.5) | collective-permute-done | bytes 32800 | tf_op jit(solution)/shard_map/ppermute | solution.py:28
  37.1 3.4 %collective-permute-start.7 = (f32[34,1,256]{2,1,0:T(1,128)S(1)}, f32[34,1,256]{2,1,0:T(1,128)S(1)}, u32[]{:S(2)}, u32[]{:S(2)}) collective-permute-start(f32[34,1,256]{2,1,0:T(1,128)S(1)} %get-tuple-element.52), channel_id=1, source_target_pairs={{1,0},{2,1},{3,2},{4,3},{5,4},{6,5},{7,6},{8,7},{9,8},{10,9},{11,1... | collective-permute-start | bytes 104456 | tf_op jit(solution)/shard_map/ppermute | solution.py:28
  40.5 3.4 %collective-permute-done.7 = f32[34,1,256]{2,1,0:T(1,128)S(1)} collective-permute-done((f32[34,1,256]{2,1,0:T(1,128)S(1)}, f32[34,1,256]{2,1,0:T(1,128)S(1)}, u32[]{:S(2)}, u32[]{:S(2)}) %collective-permute-start.7) | collective-permute-done | bytes 34848 | tf_op jit(solution)/shard_map/ppermute | solution.py:28
  47.6 3.1 collective-permute-start.8
  52.6 3.3 %collective-permute-done.9 = f32[1,32,256]{2,1,0:T(8,128)S(1)} collective-permute-done((f32[1,32,256]{2,1,0:T(8,128)S(1)}, f32[1,32,256]{2,1,0:T(8,128)S(1)}, u32[]{:S(2)}, u32[]{:S(2)}) %collective-permute-start.9) | collective-permute-done | bytes 32800 | tf_op jit(solution)/shard_map/ppermute | solution.py:28
  57.8 3.4 %collective-permute-start.11 = (f32[34,1,256]{2,1,0:T(1,128)S(1)}, f32[34,1,256]{2,1,0:T(1,128)S(1)}, u32[]{:S(2)}, u32[]{:S(2)}) collective-permute-start(f32[34,1,256]{2,1,0:T(1,128)S(1)} %get-tuple-element.50), channel_id=1, source_target_pairs={{1,0},{2,1},{3,2},{4,3},{5,4},{6,5},{7,6},{8,7},{9,8},{10,9},{11,1... | collective-permute-start | bytes 104456 | tf_op jit(solution)/shard_map/ppermute | solution.py:28
  61.2 3.4 %collective-permute-done.11 = f32[34,1,256]{2,1,0:T(1,128)S(1)} collective-permute-done((f32[34,1,256]{2,1,0:T(1,128)S(1)}, f32[34,1,256]{2,1,0:T(1,128)S(1)}, u32[]{:S(2)}, u32[]{:S(2)}) %collective-permute-start.11) | collective-permute-done | bytes 34848 | tf_op jit(solution)/shard_map/ppermute | solution.py:28
  68.3 3.1 collective-permute-start.12
  73.3 3.3 %collective-permute-done.13 = f32[1,32,256]{2,1,0:T(8,128)S(1)} collective-permute-done((f32[1,32,256]{2,1,0:T(8,128)S(1)}, f32[1,32,256]{2,1,0:T(8,128)S(1)}, u32[]{:S(2)}, u32[]{:S(2)}) %collective-permute-start.13) | collective-permute-done | bytes 32800 | tf_op jit(solution)/shard_map/ppermute | solution.py:28
  78.6 3.4 %collective-permute-start.15 = (f32[34,1,256]{2,1,0:T(1,128)S(1)}, f32[34,1,256]{2,1,0:T(1,128)S(1)}, u32[]{:S(2)}, u32[]{:S(2)}) collective-permute-start(f32[34,1,256]{2,1,0:T(1,128)S(1)} %get-tuple-element.48), channel_id=1, source_target_pairs={{1,0},{2,1},{3,2},{4,3},{5,4},{6,5},{7,6},{8,7},{9,8},{10,9},{11,1... | collective-permute-start | bytes 104456 | tf_op jit(solution)/shard_map/ppermute | solution.py:28
  82.0 3.4 %collective-permute-done.15 = f32[34,1,256]{2,1,0:T(1,128)S(1)} collective-permute-done((f32[34,1,256]{2,1,0:T(1,128)S(1)}, f32[34,1,256]{2,1,0:T(1,128)S(1)}, u32[]{:S(2)}, u32[]{:S(2)}) %collective-permute-start.15) | collective-permute-done | bytes 34848 | tf_op jit(solution)/shard_map/ppermute | solution.py:28
  86.4 3.3 %multiply_reduce_fusion.2 = (f32[]{:T(128)}, f32[]{:T(128)}, f32[32,32,256]{2,1,0:T(8,128)S(1)}) fusion(f32[32,32,256]{2,1,0:T(8,128)S(1)} %fusion.98, f32[32,32,256]{2,1,0:T(8,128)S(1)} %copy-done.20, f32[32,32,256]{2,1,0:T(8,128)S(1)} %get-tuple-element.34, f32[34,34,258]{2,1,0:T(8,128)S(1)} %select_maximum_fusion.24, ...), kind=kLoop, calls=%fused_computation.262 | loop fusion | flops 7864318 | bytes 11669512 | tf_op jit(solution)/shard_map/reduce_sum | solution.py:103
  90.5 3.1 collective-permute-start.16
  95.5 3.3 %collective-permute-done.17 = f32[1,32,256]{2,1,0:T(8,128)S(1)} collective-permute-done((f32[1,32,256]{2,1,0:T(8,128)S(1)}, f32[1,32,256]{2,1,0:T(8,128)S(1)}, u32[]{:S(2)}, u32[]{:S(2)}) %collective-permute-start.17) | collective-permute-done | bytes 32800 | tf_op jit(solution)/shard_map/ppermute | solution.py:28
  100.7 3.5 %collective-permute-start.19 = (f32[34,1,256]{2,1,0:T(1,128)S(1)}, f32[34,1,256]{2,1,0:T(1,128)S(1)}, u32[]{:S(2)}, u32[]{:S(2)}) collective-permute-start(f32[34,1,256]{2,1,0:T(1,128)S(1)} %get-tuple-element.46), channel_id=1, source_target_pairs={{1,0},{2,1},{3,2},{4,3},{5,4},{6,5},{7,6},{8,7},{9,8},{10,9},{11,1... | collective-permute-start | bytes 104456 | tf_op jit(solution)/shard_map/ppermute | solution.py:28
  104.3 3.2 collective-permute-done.19
  111.2 3.1 collective-permute-start.20
  116.2 3.3 %collective-permute-done.21 = f32[1,32,256]{2,1,0:T(8,128)S(1)} collective-permute-done((f32[1,32,256]{2,1,0:T(8,128)S(1)}, f32[1,32,256]{2,1,0:T(8,128)S(1)}, u32[]{:S(2)}, u32[]{:S(2)}) %collective-permute-start.21) | collective-permute-done | bytes 32800 | tf_op jit(solution)/shard_map/ppermute | solution.py:28
  121.5 3.4 %collective-permute-start.23 = (f32[34,1,256]{2,1,0:T(1,128)S(1)}, f32[34,1,256]{2,1,0:T(1,128)S(1)}, u32[]{:S(2)}, u32[]{:S(2)}) collective-permute-start(f32[34,1,256]{2,1,0:T(1,128)S(1)} %get-tuple-element.44), channel_id=1, source_target_pairs={{1,0},{2,1},{3,2},{4,3},{5,4},{6,5},{7,6},{8,7},{9,8},{10,9},{11,1... | collective-permute-start | bytes 104456 | tf_op jit(solution)/shard_map/ppermute | solution.py:28
  124.8 3.4 %collective-permute-done.23 = f32[34,1,256]{2,1,0:T(1,128)S(1)} collective-permute-done((f32[34,1,256]{2,1,0:T(1,128)S(1)}, f32[34,1,256]{2,1,0:T(1,128)S(1)}, u32[]{:S(2)}, u32[]{:S(2)}) %collective-permute-start.23) | collective-permute-done | bytes 34848 | tf_op jit(solution)/shard_map/ppermute | solution.py:28
  129.2 2.7 fusion.59
  132.0 3.1 collective-permute-start.24
  137.0 3.3 %collective-permute-done.25 = f32[1,32,256]{2,1,0:T(8,128)S(1)} collective-permute-done((f32[1,32,256]{2,1,0:T(8,128)S(1)}, f32[1,32,256]{2,1,0:T(8,128)S(1)}, u32[]{:S(2)}, u32[]{:S(2)}) %collective-permute-start.25) | collective-permute-done | bytes 32800 | tf_op jit(solution)/shard_map/ppermute | solution.py:28
  142.3 3.4 %collective-permute-start.27 = (f32[34,1,256]{2,1,0:T(1,128)S(1)}, f32[34,1,256]{2,1,0:T(1,128)S(1)}, u32[]{:S(2)}, u32[]{:S(2)}) collective-permute-start(f32[34,1,256]{2,1,0:T(1,128)S(1)} %get-tuple-element.42), channel_id=1, source_target_pairs={{1,0},{2,1},{3,2},{4,3},{5,4},{6,5},{7,6},{8,7},{9,8},{10,9},{11,1... | collective-permute-start | bytes 104456 | tf_op jit(solution)/shard_map/ppermute | solution.py:28
  145.7 11.9 %all-reduce.13 = (f32[]{:T(128)}, f32[]{:T(128)}) all-reduce(f32[]{:T(128)} %get-tuple-element.7, f32[]{:T(128)} %get-tuple-element.6), channel_id=1, replica_groups=mesh['gx'=8,'gy'=16] {'gx'}, use_global_device_ids=true, to_apply=%region_1.2 | all-reduce | flops 2 | bytes 16 | tf_op jit(solution)/shard_map/psum | solution.py:101
  157.5 24.4 %all-reduce.11 = (f32[]{:T(128)}, f32[]{:T(128)}) all-reduce(f32[]{:T(128)} %get-tuple-element.14, f32[]{:T(128)} %get-tuple-element.15), channel_id=1, replica_groups=mesh['gx'=8,'gy'=16] {'gy'}, use_global_device_ids=true, to_apply=%region_2.3 | all-reduce | flops 2 | bytes 16 | tf_op jit(solution)/shard_map/psum | solution.py:101
  185.7 6.6 %fusion.125 = (f32[32,32,256]{2,1,0:T(8,128)S(1)}, f32[32,32,256]{2,1,0:T(8,128)S(1)}, f32[32,32,256]{2,1,0:T(8,128)}) fusion(f32[32,32,256]{2,1,0:T(8,128)S(1)} %copy-done.7, f32[32,32,256]{2,1,0:T(8,128)S(1)} %copy-done.4, f32[32,32,256]{2,1,0:T(8,128)S(1)} %copy-done.1, f32[32,32,256]{2,1,0:T(8,128)S(1)} %get-tuple-element.31, ...), kind=kLoop, calls=%fused_computation.275 | loop fusion | flops 7864320 | bytes 13766660 | tf_op jit(solution)/shard_map/mul | solution.py:84
  192.3 10.5 %collective-permute-start.28 = (f32[1,32,256]{2,1,0:T(8,128)S(1)}, f32[1,32,256]{2,1,0:T(8,128)S(1)}, u32[]{:S(2)}, u32[]{:S(2)}) collective-permute-start(f32[1,32,256]{2,1,0:T(8,128)S(1)} %get-tuple-element.59), channel_id=1, source_target_pairs={{0,16},{16,32},{32,48},{48,64},{64,80},{80,96},{96,112},{1,17},{17... | collective-permute-start | bytes 98312 | tf_op jit(solution)/shard_map/ppermute | solution.py:25
  204.8 3.3 %collective-permute-done.29 = f32[1,32,256]{2,1,0:T(8,128)S(1)} collective-permute-done((f32[1,32,256]{2,1,0:T(8,128)S(1)}, f32[1,32,256]{2,1,0:T(8,128)S(1)}, u32[]{:S(2)}, u32[]{:S(2)}) %collective-permute-start.29) | collective-permute-done | bytes 32800 | tf_op jit(solution)/shard_map/ppermute | solution.py:28
  208.2 5.5 %collective-permute-start.30 = (f32[34,1,256]{2,1,0:T(1,128)S(1)}, f32[34,1,256]{2,1,0:T(1,128)S(1)}, u32[]{:S(2)}, u32[]{:S(2)}) collective-permute-start(f32[34,1,256]{2,1,0:T(1,128)S(1)} %get-tuple-element.39), channel_id=1, source_target_pairs={{0,1},{1,2},{2,3},{3,4},{4,5},{5,6},{6,7},{7,8},{8,9},{9,10},{10,1... | collective-permute-start | bytes 104456 | tf_op jit(solution)/shard_map/ppermute | solution.py:25
  215.6 4.9 %collective-permute-done.31 = f32[34,1,256]{2,1,0:T(1,128)S(1)} collective-permute-done((f32[34,1,256]{2,1,0:T(1,128)S(1)}, f32[34,1,256]{2,1,0:T(1,128)S(1)}, u32[]{:S(2)}, u32[]{:S(2)}) %collective-permute-start.31) | collective-permute-done | bytes 34848 | tf_op jit(solution)/shard_map/ppermute | solution.py:28
  221.4 3.5 %fusion.128 = (f32[32,32,256]{2,1,0:T(8,128)S(1)}, f32[32,32,256]{2,1,0:T(8,128)}) fusion(f32[32,32,256]{2,1,0:T(8,128)S(1)} %get-tuple-element.20, f32[32,32,256]{2,1,0:T(8,128)S(1)} %get-tuple-element.21, f32[32,32,256]{2,1,0:T(8,128)S(1)} %copy-done.7, f32[34,34,258]{2,1,0:T(8,128)S(1)} %select_maximum_fusion.8, f32[32,32,256]{2,1,0:T(8,128)S(1)} %copy-done.4, ...), kind=kLoop, calls=%fused_computation.307 | loop fusion | flops 8650752 | bytes 12718080 | tf_op jit(solution)/shard_map/add | solution.py:86
  224.9 3.5 %collective-permute-start.32 = (f32[1,32,256]{2,1,0:T(8,128)S(1)}, f32[1,32,256]{2,1,0:T(8,128)S(1)}, u32[]{:S(2)}, u32[]{:S(2)}) collective-permute-start(f32[1,32,256]{2,1,0:T(8,128)S(1)} %get-tuple-element.57), channel_id=1, source_target_pairs={{0,16},{16,32},{32,48},{48,64},{64,80},{80,96},{96,112},{1,17},{17... | collective-permute-start | bytes 98312 | tf_op jit(solution)/shard_map/ppermute | solution.py:25
  230.4 3.3 %collective-permute-done.33 = f32[1,32,256]{2,1,0:T(8,128)S(1)} collective-permute-done((f32[1,32,256]{2,1,0:T(8,128)S(1)}, f32[1,32,256]{2,1,0:T(8,128)S(1)}, u32[]{:S(2)}, u32[]{:S(2)}) %collective-permute-start.33) | collective-permute-done | bytes 32800 | tf_op jit(solution)/shard_map/ppermute | solution.py:28
  235.7 3.4 %collective-permute-start.35 = (f32[34,1,256]{2,1,0:T(1,128)S(1)}, f32[34,1,256]{2,1,0:T(1,128)S(1)}, u32[]{:S(2)}, u32[]{:S(2)}) collective-permute-start(f32[34,1,256]{2,1,0:T(1,128)S(1)} %get-tuple-element.38), channel_id=1, source_target_pairs={{1,0},{2,1},{3,2},{4,3},{5,4},{6,5},{7,6},{8,7},{9,8},{10,9},{11,1... | collective-permute-start | bytes 104456 | tf_op jit(solution)/shard_map/ppermute | solution.py:28
  240.3 10.9 %all-reduce.12 = (f32[]{:T(128)}, f32[]{:T(128)}) all-reduce(f32[]{:T(128)} %get-tuple-element.5, f32[]{:T(128)} %get-tuple-element.4), channel_id=1, replica_groups=mesh['gx'=8,'gy'=16] {'gx'}, use_global_device_ids=true, to_apply=%region_7.8 | all-reduce | flops 2 | bytes 16 | tf_op jit(solution)/shard_map/psum | solution.py:101
  251.2 24.6 %all-reduce.10 = (f32[]{:T(128)}, f32[]{:T(128)}) all-reduce(f32[]{:T(128)} %get-tuple-element.12, f32[]{:T(128)} %get-tuple-element.13), channel_id=1, replica_groups=mesh['gx'=8,'gy'=16] {'gy'}, use_global_device_ids=true, to_apply=%region_8.9 | all-reduce | flops 2 | bytes 16 | tf_op jit(solution)/shard_map/psum | solution.py:101
  282.9 7.4 %multiply_subtract_fusion = (f32[32,32,256]{2,1,0:T(8,128)}, f32[32,32,256]{2,1,0:T(8,128)S(1)}) fusion(f32[32,32,256]{2,1,0:T(8,128)} %copy-done.9, f32[]{:T(128)S(6)} %div.70, f32[]{:T(128)S(6)} %div.72, f32[32,32,256]{2,1,0:T(8,128)} %copy-done.12, f32[]{:T(128)S(6)} %div.66, f32[32,32,256]{2,1,0:T(8,128)} %copy-done.23, f32[32,32,256]{2,1,0:T(8,128)} %copy-done.18, ...), kind=kLoop, calls=%fused_computation.254 | loop fusion | flops 9961472 | bytes 15863820 | tf_op jit(solution)/shard_map/sub | solution.py:121
  290.3 10.8 %collective-permute-start.36 = (f32[1,32,256]{2,1,0:T(8,128)S(1)}, f32[1,32,256]{2,1,0:T(8,128)S(1)}, u32[]{:S(2)}, u32[]{:S(2)}) collective-permute-start(f32[1,32,256]{2,1,0:T(8,128)S(1)} %get-tuple-element.55), channel_id=1, source_target_pairs={{0,16},{16,32},{32,48},{48,64},{64,80},{80,96},{96,112},{1,17},{17... | collective-permute-start | bytes 98312 | tf_op jit(solution)/shard_map/ppermute | solution.py:25
  303.5 2.9 collective-permute-done.37
  306.4 5.6 %collective-permute-start.38 = (f32[34,1,256]{2,1,0:T(1,128)S(1)}, f32[34,1,256]{2,1,0:T(1,128)S(1)}, u32[]{:S(2)}, u32[]{:S(2)}) collective-permute-start(f32[34,1,256]{2,1,0:T(1,128)S(1)} %get-tuple-element.35), channel_id=1, source_target_pairs={{0,1},{1,2},{2,3},{3,4},{4,5},{5,6},{6,7},{7,8},{8,9},{9,10},{10,1... | collective-permute-start | bytes 104456 | tf_op jit(solution)/shard_map/ppermute | solution.py:25
  316.0 2.9 collective-permute-done.39
  319.8 3.5 %fusion.5 = f32[32,32,256]{2,1,0:T(8,128)} fusion(f32[32,32,256]{2,1,0:T(8,128)S(1)} %copy-done.19, f32[32,32,256]{2,1,0:T(8,128)S(1)} %copy-done.8, f32[34,34,258]{2,1,0:T(8,128)S(1)} %select_maximum_fusion, f32[32,32,256]{2,1,0:T(8,128)S(1)} %copy-done.5, f32[32,32,256]{2,1,0:T(8,128)S(1)} %copy-done.2, f32[34,1,256]{2,1,0:T(1,128)S(1)} %collective-permute-done.39, ...), kind=kLoop, calls=%fused_computation.49 | loop fusion | flops 7864320 | bytes 12718088 | tf_op jit(solution)/shard_map/sub | solution.py:122
  (136 shorter events, 69.9 us)
Async XLA Ops:
  1.4 5.7 %collective-permute-start = (s32[1,32,256]{2,1,0:T(8,128)S(1)}, s32[1,32,256]{2,1,0:T(8,128)S(1)}, u32[]{:S(2)}, u32[]{:S(2)}) collective-permute-start(s32[1,32,256]{2,1,0:T(8,128)S(1)} %get-tuple-element.74), channel_id=1, source_target_pairs={{0,16},{16,32},{32,48},{48,64},{64,80},{80,96},{96,112},{1,17},{17... | collective-permute-start | bytes 98312 | tf_op jit(solution)/shard_map/ppermute | solution.py:25
  5.2 5.2 %collective-permute-start.1 = (s32[1,32,256]{2,1,0:T(8,128)S(1)}, s32[1,32,256]{2,1,0:T(8,128)S(1)}, u32[]{:S(2)}, u32[]{:S(2)}) collective-permute-start(s32[1,32,256]{2,1,0:T(8,128)S(1)} %get-tuple-element.73), channel_id=1, source_target_pairs={{16,0},{32,16},{48,32},{64,48},{80,64},{96,80},{112,96},{17,1},{33... | collective-permute-start | bytes 98312 | tf_op jit(solution)/shard_map/ppermute | solution.py:28
  10.5 6.0 %collective-permute-start.2 = (s32[34,1,256]{2,1,0:T(1,128)S(1)}, s32[34,1,256]{2,1,0:T(1,128)S(1)}, u32[]{:S(2)}, u32[]{:S(2)}) collective-permute-start(s32[34,1,256]{2,1,0:T(1,128)S(1)} %get-tuple-element.53), channel_id=1, source_target_pairs={{0,1},{1,2},{2,3},{3,4},{4,5},{5,6},{6,7},{7,8},{8,9},{9,10},{10,1... | collective-permute-start | bytes 104456 | tf_op jit(solution)/shard_map/ppermute | solution.py:25
  13.9 6.8 %collective-permute-start.3 = (s32[34,1,256]{2,1,0:T(1,128)S(1)}, s32[34,1,256]{2,1,0:T(1,128)S(1)}, u32[]{:S(2)}, u32[]{:S(2)}) collective-permute-start(s32[34,1,256]{2,1,0:T(1,128)S(1)} %get-tuple-element.54), channel_id=1, source_target_pairs={{1,0},{2,1},{3,2},{4,3},{5,4},{6,5},{7,6},{8,7},{9,8},{10,9},{11,1... | collective-permute-start | bytes 104456 | tf_op jit(solution)/shard_map/ppermute | solution.py:28
  26.5 102.7 %copy-start = (f32[32,32,256]{2,1,0:T(8,128)}, f32[32,32,256]{2,1,0:T(8,128)S(1)}, u32[]{:S(2)}) copy-start(f32[32,32,256]{2,1,0:T(8,128)S(1)} %get-tuple-element.32) | copy-start | bytes 3145732
  26.5 102.7 %copy-start.3 = (f32[32,32,256]{2,1,0:T(8,128)}, f32[32,32,256]{2,1,0:T(8,128)S(1)}, u32[]{:S(2)}) copy-start(f32[32,32,256]{2,1,0:T(8,128)S(1)} %get-tuple-element.33) | copy-start | bytes 3145732
  26.5 102.7 %copy-start.6 = (f32[32,32,256]{2,1,0:T(8,128)}, f32[32,32,256]{2,1,0:T(8,128)S(1)}, u32[]{:S(2)}) copy-start(f32[32,32,256]{2,1,0:T(8,128)S(1)} %get-tuple-element.34) | copy-start | bytes 3145732
  26.5 5.3 %collective-permute-start.4 = (f32[1,32,256]{2,1,0:T(8,128)S(1)}, f32[1,32,256]{2,1,0:T(8,128)S(1)}, u32[]{:S(2)}, u32[]{:S(2)}) collective-permute-start(f32[1,32,256]{2,1,0:T(8,128)S(1)} %get-tuple-element.71), channel_id=1, source_target_pairs={{0,16},{16,32},{32,48},{48,64},{64,80},{80,96},{96,112},{1,17},{17... | collective-permute-start | bytes 98312 | tf_op jit(solution)/shard_map/ppermute | solution.py:25
  29.9 5.2 %collective-permute-start.5 = (f32[1,32,256]{2,1,0:T(8,128)S(1)}, f32[1,32,256]{2,1,0:T(8,128)S(1)}, u32[]{:S(2)}, u32[]{:S(2)}) collective-permute-start(f32[1,32,256]{2,1,0:T(8,128)S(1)} %get-tuple-element.72), channel_id=1, source_target_pairs={{16,0},{32,16},{48,32},{64,48},{80,64},{96,80},{112,96},{17,1},{33... | collective-permute-start | bytes 98312 | tf_op jit(solution)/shard_map/ppermute | solution.py:28
  35.2 5.3 %collective-permute-start.6 = (f32[34,1,256]{2,1,0:T(1,128)S(1)}, f32[34,1,256]{2,1,0:T(1,128)S(1)}, u32[]{:S(2)}, u32[]{:S(2)}) collective-permute-start(f32[34,1,256]{2,1,0:T(1,128)S(1)} %get-tuple-element.51), channel_id=1, source_target_pairs={{0,1},{1,2},{2,3},{3,4},{4,5},{5,6},{6,7},{7,8},{8,9},{9,10},{10,1... | collective-permute-start | bytes 104456 | tf_op jit(solution)/shard_map/ppermute | solution.py:25
  37.1 6.8 %collective-permute-start.7 = (f32[34,1,256]{2,1,0:T(1,128)S(1)}, f32[34,1,256]{2,1,0:T(1,128)S(1)}, u32[]{:S(2)}, u32[]{:S(2)}) collective-permute-start(f32[34,1,256]{2,1,0:T(1,128)S(1)} %get-tuple-element.52), channel_id=1, source_target_pairs={{1,0},{2,1},{3,2},{4,3},{5,4},{6,5},{7,6},{8,7},{9,8},{10,9},{11,1... | collective-permute-start | bytes 104456 | tf_op jit(solution)/shard_map/ppermute | solution.py:28
  47.6 5.0 %collective-permute-start.8 = (f32[1,32,256]{2,1,0:T(8,128)S(1)}, f32[1,32,256]{2,1,0:T(8,128)S(1)}, u32[]{:S(2)}, u32[]{:S(2)}) collective-permute-start(f32[1,32,256]{2,1,0:T(8,128)S(1)} %get-tuple-element.69), channel_id=1, source_target_pairs={{0,16},{16,32},{32,48},{48,64},{64,80},{80,96},{96,112},{1,17},{17... | collective-permute-start | bytes 98312 | tf_op jit(solution)/shard_map/ppermute | solution.py:25
  50.6 5.2 %collective-permute-start.9 = (f32[1,32,256]{2,1,0:T(8,128)S(1)}, f32[1,32,256]{2,1,0:T(8,128)S(1)}, u32[]{:S(2)}, u32[]{:S(2)}) collective-permute-start(f32[1,32,256]{2,1,0:T(8,128)S(1)} %get-tuple-element.70), channel_id=1, source_target_pairs={{16,0},{32,16},{48,32},{64,48},{80,64},{96,80},{112,96},{17,1},{33... | collective-permute-start | bytes 98312 | tf_op jit(solution)/shard_map/ppermute | solution.py:28
  55.9 5.3 %collective-permute-start.10 = (f32[34,1,256]{2,1,0:T(1,128)S(1)}, f32[34,1,256]{2,1,0:T(1,128)S(1)}, u32[]{:S(2)}, u32[]{:S(2)}) collective-permute-start(f32[34,1,256]{2,1,0:T(1,128)S(1)} %get-tuple-element.49), channel_id=1, source_target_pairs={{0,1},{1,2},{2,3},{3,4},{4,5},{5,6},{6,7},{7,8},{8,9},{9,10},{10,1... | collective-permute-start | bytes 104456 | tf_op jit(solution)/shard_map/ppermute | solution.py:25
  57.8 6.8 %collective-permute-start.11 = (f32[34,1,256]{2,1,0:T(1,128)S(1)}, f32[34,1,256]{2,1,0:T(1,128)S(1)}, u32[]{:S(2)}, u32[]{:S(2)}) collective-permute-start(f32[34,1,256]{2,1,0:T(1,128)S(1)} %get-tuple-element.50), channel_id=1, source_target_pairs={{1,0},{2,1},{3,2},{4,3},{5,4},{6,5},{7,6},{8,7},{9,8},{10,9},{11,1... | collective-permute-start | bytes 104456 | tf_op jit(solution)/shard_map/ppermute | solution.py:28
  68.3 5.0 %collective-permute-start.12 = (f32[1,32,256]{2,1,0:T(8,128)S(1)}, f32[1,32,256]{2,1,0:T(8,128)S(1)}, u32[]{:S(2)}, u32[]{:S(2)}) collective-permute-start(f32[1,32,256]{2,1,0:T(8,128)S(1)} %get-tuple-element.67), channel_id=1, source_target_pairs={{0,16},{16,32},{32,48},{48,64},{64,80},{80,96},{96,112},{1,17},{17... | collective-permute-start | bytes 98312 | tf_op jit(solution)/shard_map/ppermute | solution.py:25
  71.4 5.2 %collective-permute-start.13 = (f32[1,32,256]{2,1,0:T(8,128)S(1)}, f32[1,32,256]{2,1,0:T(8,128)S(1)}, u32[]{:S(2)}, u32[]{:S(2)}) collective-permute-start(f32[1,32,256]{2,1,0:T(8,128)S(1)} %get-tuple-element.68), channel_id=1, source_target_pairs={{16,0},{32,16},{48,32},{64,48},{80,64},{96,80},{112,96},{17,1},{33... | collective-permute-start | bytes 98312 | tf_op jit(solution)/shard_map/ppermute | solution.py:28
  76.7 5.3 %collective-permute-start.14 = (f32[34,1,256]{2,1,0:T(1,128)S(1)}, f32[34,1,256]{2,1,0:T(1,128)S(1)}, u32[]{:S(2)}, u32[]{:S(2)}) collective-permute-start(f32[34,1,256]{2,1,0:T(1,128)S(1)} %get-tuple-element.47), channel_id=1, source_target_pairs={{0,1},{1,2},{2,3},{3,4},{4,5},{5,6},{6,7},{7,8},{8,9},{9,10},{10,1... | collective-permute-start | bytes 104456 | tf_op jit(solution)/shard_map/ppermute | solution.py:25
  78.6 6.8 %collective-permute-start.15 = (f32[34,1,256]{2,1,0:T(1,128)S(1)}, f32[34,1,256]{2,1,0:T(1,128)S(1)}, u32[]{:S(2)}, u32[]{:S(2)}) collective-permute-start(f32[34,1,256]{2,1,0:T(1,128)S(1)} %get-tuple-element.48), channel_id=1, source_target_pairs={{1,0},{2,1},{3,2},{4,3},{5,4},{6,5},{7,6},{8,7},{9,8},{10,9},{11,1... | collective-permute-start | bytes 104456 | tf_op jit(solution)/shard_map/ppermute | solution.py:28
  89.6 39.6 %copy-start.15 = (f32[32,32,256]{2,1,0:T(8,128)}, f32[32,32,256]{2,1,0:T(8,128)S(1)}, u32[]{:S(2)}) copy-start(f32[32,32,256]{2,1,0:T(8,128)S(1)} %get-tuple-element.23) | copy-start | bytes 3145732
  90.5 5.0 %collective-permute-start.16 = (f32[1,32,256]{2,1,0:T(8,128)S(1)}, f32[1,32,256]{2,1,0:T(8,128)S(1)}, u32[]{:S(2)}, u32[]{:S(2)}) collective-permute-start(f32[1,32,256]{2,1,0:T(8,128)S(1)} %get-tuple-element.65), channel_id=1, source_target_pairs={{0,16},{16,32},{32,48},{48,64},{64,80},{80,96},{96,112},{1,17},{17... | collective-permute-start | bytes 98312 | tf_op jit(solution)/shard_map/ppermute | solution.py:25
  93.5 5.2 %collective-permute-start.17 = (f32[1,32,256]{2,1,0:T(8,128)S(1)}, f32[1,32,256]{2,1,0:T(8,128)S(1)}, u32[]{:S(2)}, u32[]{:S(2)}) collective-permute-start(f32[1,32,256]{2,1,0:T(8,128)S(1)} %get-tuple-element.66), channel_id=1, source_target_pairs={{16,0},{32,16},{48,32},{64,48},{80,64},{96,80},{112,96},{17,1},{33... | collective-permute-start | bytes 98312 | tf_op jit(solution)/shard_map/ppermute | solution.py:28
  98.8 5.5 %collective-permute-start.18 = (f32[34,1,256]{2,1,0:T(1,128)S(1)}, f32[34,1,256]{2,1,0:T(1,128)S(1)}, u32[]{:S(2)}, u32[]{:S(2)}) collective-permute-start(f32[34,1,256]{2,1,0:T(1,128)S(1)} %get-tuple-element.45), channel_id=1, source_target_pairs={{0,1},{1,2},{2,3},{3,4},{4,5},{5,6},{6,7},{7,8},{8,9},{9,10},{10,1... | collective-permute-start | bytes 104456 | tf_op jit(solution)/shard_map/ppermute | solution.py:25
  100.7 6.8 %collective-permute-start.19 = (f32[34,1,256]{2,1,0:T(1,128)S(1)}, f32[34,1,256]{2,1,0:T(1,128)S(1)}, u32[]{:S(2)}, u32[]{:S(2)}) collective-permute-start(f32[34,1,256]{2,1,0:T(1,128)S(1)} %get-tuple-element.46), channel_id=1, source_target_pairs={{1,0},{2,1},{3,2},{4,3},{5,4},{6,5},{7,6},{8,7},{9,8},{10,9},{11,1... | collective-permute-start | bytes 104456 | tf_op jit(solution)/shard_map/ppermute | solution.py:28
  111.2 5.0 %collective-permute-start.20 = (f32[1,32,256]{2,1,0:T(8,128)S(1)}, f32[1,32,256]{2,1,0:T(8,128)S(1)}, u32[]{:S(2)}, u32[]{:S(2)}) collective-permute-start(f32[1,32,256]{2,1,0:T(8,128)S(1)} %get-tuple-element.63), channel_id=1, source_target_pairs={{0,16},{16,32},{32,48},{48,64},{64,80},{80,96},{96,112},{1,17},{17... | collective-permute-start | bytes 98312 | tf_op jit(solution)/shard_map/ppermute | solution.py:25
  114.3 5.2 %collective-permute-start.21 = (f32[1,32,256]{2,1,0:T(8,128)S(1)}, f32[1,32,256]{2,1,0:T(8,128)S(1)}, u32[]{:S(2)}, u32[]{:S(2)}) collective-permute-start(f32[1,32,256]{2,1,0:T(8,128)S(1)} %get-tuple-element.64), channel_id=1, source_target_pairs={{16,0},{32,16},{48,32},{64,48},{80,64},{96,80},{112,96},{17,1},{33... | collective-permute-start | bytes 98312 | tf_op jit(solution)/shard_map/ppermute | solution.py:28
  119.5 5.3 %collective-permute-start.22 = (f32[34,1,256]{2,1,0:T(1,128)S(1)}, f32[34,1,256]{2,1,0:T(1,128)S(1)}, u32[]{:S(2)}, u32[]{:S(2)}) collective-permute-start(f32[34,1,256]{2,1,0:T(1,128)S(1)} %get-tuple-element.43), channel_id=1, source_target_pairs={{0,1},{1,2},{2,3},{3,4},{4,5},{5,6},{6,7},{7,8},{8,9},{9,10},{10,1... | collective-permute-start | bytes 104456 | tf_op jit(solution)/shard_map/ppermute | solution.py:25
  121.5 6.8 %collective-permute-start.23 = (f32[34,1,256]{2,1,0:T(1,128)S(1)}, f32[34,1,256]{2,1,0:T(1,128)S(1)}, u32[]{:S(2)}, u32[]{:S(2)}) collective-permute-start(f32[34,1,256]{2,1,0:T(1,128)S(1)} %get-tuple-element.44), channel_id=1, source_target_pairs={{1,0},{2,1},{3,2},{4,3},{5,4},{6,5},{7,6},{8,7},{9,8},{10,9},{11,1... | collective-permute-start | bytes 104456 | tf_op jit(solution)/shard_map/ppermute | solution.py:28
  132.0 5.0 %collective-permute-start.24 = (f32[1,32,256]{2,1,0:T(8,128)S(1)}, f32[1,32,256]{2,1,0:T(8,128)S(1)}, u32[]{:S(2)}, u32[]{:S(2)}) collective-permute-start(f32[1,32,256]{2,1,0:T(8,128)S(1)} %get-tuple-element.61), channel_id=1, source_target_pairs={{0,16},{16,32},{32,48},{48,64},{64,80},{80,96},{96,112},{1,17},{17... | collective-permute-start | bytes 98312 | tf_op jit(solution)/shard_map/ppermute | solution.py:25
  135.1 5.2 %collective-permute-start.25 = (f32[1,32,256]{2,1,0:T(8,128)S(1)}, f32[1,32,256]{2,1,0:T(8,128)S(1)}, u32[]{:S(2)}, u32[]{:S(2)}) collective-permute-start(f32[1,32,256]{2,1,0:T(8,128)S(1)} %get-tuple-element.62), channel_id=1, source_target_pairs={{16,0},{32,16},{48,32},{64,48},{80,64},{96,80},{112,96},{17,1},{33... | collective-permute-start | bytes 98312 | tf_op jit(solution)/shard_map/ppermute | solution.py:28
  140.4 43.0 %collective-permute-start.26 = (f32[34,1,256]{2,1,0:T(1,128)S(1)}, f32[34,1,256]{2,1,0:T(1,128)S(1)}, u32[]{:S(2)}, u32[]{:S(2)}) collective-permute-start(f32[34,1,256]{2,1,0:T(1,128)S(1)} %get-tuple-element.41), channel_id=1, source_target_pairs={{0,1},{1,2},{2,3},{3,4},{4,5},{5,6},{6,7},{7,8},{8,9},{9,10},{10,1... | collective-permute-start | bytes 104456 | tf_op jit(solution)/shard_map/ppermute | solution.py:25
  142.3 41.1 %collective-permute-start.27 = (f32[34,1,256]{2,1,0:T(1,128)S(1)}, f32[34,1,256]{2,1,0:T(1,128)S(1)}, u32[]{:S(2)}, u32[]{:S(2)}) collective-permute-start(f32[34,1,256]{2,1,0:T(1,128)S(1)} %get-tuple-element.42), channel_id=1, source_target_pairs={{1,0},{2,1},{3,2},{4,3},{5,4},{6,5},{7,6},{8,7},{9,8},{10,9},{11,1... | collective-permute-start | bytes 104456 | tf_op jit(solution)/shard_map/ppermute | solution.py:28
  192.3 46.7 %copy-start.18 = (f32[32,32,256]{2,1,0:T(8,128)}, f32[32,32,256]{2,1,0:T(8,128)S(1)}, u32[]{:S(2)}) copy-start(f32[32,32,256]{2,1,0:T(8,128)S(1)} %get-tuple-element.21) | copy-start | bytes 3145732
  192.3 12.5 %collective-permute-start.28 = (f32[1,32,256]{2,1,0:T(8,128)S(1)}, f32[1,32,256]{2,1,0:T(8,128)S(1)}, u32[]{:S(2)}, u32[]{:S(2)}) collective-permute-start(f32[1,32,256]{2,1,0:T(8,128)S(1)} %get-tuple-element.59), channel_id=1, source_target_pairs={{0,16},{16,32},{32,48},{48,64},{64,80},{80,96},{96,112},{1,17},{17... | collective-permute-start | bytes 98312 | tf_op jit(solution)/shard_map/ppermute | solution.py:25
  202.9 5.2 %collective-permute-start.29 = (f32[1,32,256]{2,1,0:T(8,128)S(1)}, f32[1,32,256]{2,1,0:T(8,128)S(1)}, u32[]{:S(2)}, u32[]{:S(2)}) collective-permute-start(f32[1,32,256]{2,1,0:T(8,128)S(1)} %get-tuple-element.60), channel_id=1, source_target_pairs={{16,0},{32,16},{48,32},{64,48},{80,64},{96,80},{112,96},{17,1},{33... | collective-permute-start | bytes 98312 | tf_op jit(solution)/shard_map/ppermute | solution.py:28
  208.2 7.4 %collective-permute-start.30 = (f32[34,1,256]{2,1,0:T(1,128)S(1)}, f32[34,1,256]{2,1,0:T(1,128)S(1)}, u32[]{:S(2)}, u32[]{:S(2)}) collective-permute-start(f32[34,1,256]{2,1,0:T(1,128)S(1)} %get-tuple-element.39), channel_id=1, source_target_pairs={{0,1},{1,2},{2,3},{3,4},{4,5},{5,6},{6,7},{7,8},{8,9},{9,10},{10,1... | collective-permute-start | bytes 104456 | tf_op jit(solution)/shard_map/ppermute | solution.py:25
  213.7 6.8 %collective-permute-start.31 = (f32[34,1,256]{2,1,0:T(1,128)S(1)}, f32[34,1,256]{2,1,0:T(1,128)S(1)}, u32[]{:S(2)}, u32[]{:S(2)}) collective-permute-start(f32[34,1,256]{2,1,0:T(1,128)S(1)} %get-tuple-element.40), channel_id=1, source_target_pairs={{1,0},{2,1},{3,2},{4,3},{5,4},{6,5},{7,6},{8,7},{9,8},{10,9},{11,1... | collective-permute-start | bytes 104456 | tf_op jit(solution)/shard_map/ppermute | solution.py:28
  224.9 5.5 %collective-permute-start.32 = (f32[1,32,256]{2,1,0:T(8,128)S(1)}, f32[1,32,256]{2,1,0:T(8,128)S(1)}, u32[]{:S(2)}, u32[]{:S(2)}) collective-permute-start(f32[1,32,256]{2,1,0:T(8,128)S(1)} %get-tuple-element.57), channel_id=1, source_target_pairs={{0,16},{16,32},{32,48},{48,64},{64,80},{80,96},{96,112},{1,17},{17... | collective-permute-start | bytes 98312 | tf_op jit(solution)/shard_map/ppermute | solution.py:25
  228.5 5.2 %collective-permute-start.33 = (f32[1,32,256]{2,1,0:T(8,128)S(1)}, f32[1,32,256]{2,1,0:T(8,128)S(1)}, u32[]{:S(2)}, u32[]{:S(2)}) collective-permute-start(f32[1,32,256]{2,1,0:T(8,128)S(1)} %get-tuple-element.58), channel_id=1, source_target_pairs={{16,0},{32,16},{48,32},{64,48},{80,64},{96,80},{112,96},{17,1},{33... | collective-permute-start | bytes 98312 | tf_op jit(solution)/shard_map/ppermute | solution.py:28
  233.8 46.7 %collective-permute-start.34 = (f32[34,1,256]{2,1,0:T(1,128)S(1)}, f32[34,1,256]{2,1,0:T(1,128)S(1)}, u32[]{:S(2)}, u32[]{:S(2)}) collective-permute-start(f32[34,1,256]{2,1,0:T(1,128)S(1)} %get-tuple-element.37), channel_id=1, source_target_pairs={{0,1},{1,2},{2,3},{3,4},{4,5},{5,6},{6,7},{7,8},{8,9},{9,10},{10,1... | collective-permute-start | bytes 104456 | tf_op jit(solution)/shard_map/ppermute | solution.py:25
  235.7 44.8 %collective-permute-start.35 = (f32[34,1,256]{2,1,0:T(1,128)S(1)}, f32[34,1,256]{2,1,0:T(1,128)S(1)}, u32[]{:S(2)}, u32[]{:S(2)}) collective-permute-start(f32[34,1,256]{2,1,0:T(1,128)S(1)} %get-tuple-element.38), channel_id=1, source_target_pairs={{1,0},{2,1},{3,2},{4,3},{5,4},{6,5},{7,6},{8,7},{9,8},{10,9},{11,1... | collective-permute-start | bytes 104456 | tf_op jit(solution)/shard_map/ppermute | solution.py:28
  282.8 31.2 %copy-start.11 = (f32[32,32,256]{2,1,0:T(8,128)S(1)}, f32[32,32,256]{2,1,0:T(8,128)}, u32[]{:S(2)}) copy-start(f32[32,32,256]{2,1,0:T(8,128)} %copy-done.9) | copy-start | bytes 3145732
  282.8 31.2 %copy-start.14 = (f32[32,32,256]{2,1,0:T(8,128)S(1)}, f32[32,32,256]{2,1,0:T(8,128)}, u32[]{:S(2)}) copy-start(f32[32,32,256]{2,1,0:T(8,128)} %copy-done.12) | copy-start | bytes 3145732
  282.8 31.2 %copy-start.17 = (f32[32,32,256]{2,1,0:T(8,128)S(1)}, f32[32,32,256]{2,1,0:T(8,128)}, u32[]{:S(2)}) copy-start(f32[32,32,256]{2,1,0:T(8,128)} %copy-done.15) | copy-start | bytes 3145732
  290.3 13.1 %collective-permute-start.36 = (f32[1,32,256]{2,1,0:T(8,128)S(1)}, f32[1,32,256]{2,1,0:T(8,128)S(1)}, u32[]{:S(2)}, u32[]{:S(2)}) collective-permute-start(f32[1,32,256]{2,1,0:T(8,128)S(1)} %get-tuple-element.55), channel_id=1, source_target_pairs={{0,16},{16,32},{32,48},{48,64},{64,80},{80,96},{96,112},{1,17},{17... | collective-permute-start | bytes 98312 | tf_op jit(solution)/shard_map/ppermute | solution.py:25
  301.1 5.2 %collective-permute-start.37 = (f32[1,32,256]{2,1,0:T(8,128)S(1)}, f32[1,32,256]{2,1,0:T(8,128)S(1)}, u32[]{:S(2)}, u32[]{:S(2)}) collective-permute-start(f32[1,32,256]{2,1,0:T(8,128)S(1)} %get-tuple-element.56), channel_id=1, source_target_pairs={{16,0},{32,16},{48,32},{64,48},{80,64},{96,80},{112,96},{17,1},{33... | collective-permute-start | bytes 98312 | tf_op jit(solution)/shard_map/ppermute | solution.py:28
  306.4 9.5 %collective-permute-start.38 = (f32[34,1,256]{2,1,0:T(1,128)S(1)}, f32[34,1,256]{2,1,0:T(1,128)S(1)}, u32[]{:S(2)}, u32[]{:S(2)}) collective-permute-start(f32[34,1,256]{2,1,0:T(1,128)S(1)} %get-tuple-element.35), channel_id=1, source_target_pairs={{0,1},{1,2},{2,3},{3,4},{4,5},{5,6},{6,7},{7,8},{8,9},{9,10},{10,1... | collective-permute-start | bytes 104456 | tf_op jit(solution)/shard_map/ppermute | solution.py:25
  312.0 6.8 %collective-permute-start.39 = (f32[34,1,256]{2,1,0:T(1,128)S(1)}, f32[34,1,256]{2,1,0:T(1,128)S(1)}, u32[]{:S(2)}, u32[]{:S(2)}) collective-permute-start(f32[34,1,256]{2,1,0:T(1,128)S(1)} %get-tuple-element.36), channel_id=1, source_target_pairs={{1,0},{2,1},{3,2},{4,3},{5,4},{6,5},{7,6},{8,7},{9,8},{10,9},{11,1... | collective-permute-start | bytes 104456 | tf_op jit(solution)/shard_map/ppermute | solution.py:28
  (18 other events, 211.3 us)
